TPU v7x, 32 devices: a whole 2x2x4 slice. The times are simulated.
32 devices in a mesh: ctx: 8 (over y, x, core), grp: 4 (over z).
Axes of the slice: x: 2, y: 2, z: 4, core: 2. Of those that a mesh axis runs over, the one named last changes fastest.
Arguments:
- window_states: bfloat16 [4, 64, 8192], P('grp'), may hold values from -6 to 6
- query_weight: bfloat16 [8192, 8192], P('grp', 'ctx'), may hold values from -0.0625 to 0.0625
- cache_keys: bfloat16 [4, 4096, 1024], P('grp', 'ctx'), may hold values from -65 to 65
- cache_values: bfloat16 [4, 4096, 1024], P('grp', 'ctx'), may hold values from -6 to 6
- kept_blocks: int32 [4, 8, 8], P('grp', None, 'ctx'), may hold values from 0 to 31, as said below
- retained_block_count: int32 [4, 8, 8], P('grp', None, 'ctx'), may hold values from 0 to 1, as said below
- decode_queries: bfloat16 [4, 4, 8, 8192], P('grp', None, 'ctx'), may hold values from -9 to 9
- tail_keys: bfloat16 [4, 8, 64, 1024], P('grp', 'ctx'), may hold values from -6 to 6
- tail_values: bfloat16 [4, 8, 64, 1024], P('grp', 'ctx'), may hold values from -6 to 6
- row_lengths: int32 [4, 8], P('grp', 'ctx'), may hold values from 2 to 61, as said below
Outputs:
- pooled_votes: float32 [4, 8, 4096], P('grp', None, 'ctx')
- decode_out: bfloat16 [4, 4, 8, 8192], P('grp', None, 'ctx')
Inputs may be any that keep to these rules, and one draw needn't show every extreme that they name: `kept_blocks`: for key head k, entry c names one block held by ctx index c, that is one of the blocks c * 4 to c * 4 + 3; it is kept only if retained_block_count[g, k, c] is 1. `retained_block_count`: in every request some device holds 1 kept blocks for every key head. `row_lengths`: 61 is reached in every request.
All inputs are finite; a program needn't handle non-finite values.
Results may differ from a plain program's by a relative error of at most 0.0019.
Values may be sent and summed in bfloat16 or wider, within the bound.
No kernel may reach another device: no remote copies, remote signals or barrier semaphores. Data moves between devices by JAX's collectives and lax.ppermute only.
A program may use at most 128 MiB of HBM per device.

v0:
```python
import functools
import math

import jax
import jax.numpy as jnp
from jax import lax
from jax.experimental import pallas as pl
from jax.experimental.pallas import tpu as pltpu
from jax.sharding import PartitionSpec as P


KEY_HEADS = 8
HEAD_DIMENSION = 128
BLOCK_POSITIONS = 128
POOL = 7
LANES = 128
NOTE_ROWS = 16


def rotary_table(positions, head_size):
    exponent = jnp.arange(0, head_size, 2).astype(jnp.float32) / head_size
    inverse = jnp.power(jnp.float32(500000.0), -exponent)
    wavelength = 2.0 * math.pi / inverse
    smooth = (8192.0 / wavelength - 1.0) / 3.0
    blended = (1.0 - smooth) * inverse / 8.0 + smooth * inverse
    adjusted = jnp.where(
        wavelength > 8192.0, inverse / 8.0, jnp.where(wavelength < 2048.0, inverse, blended)
    )
    angles = positions[:, None] * adjusted[None, :]
    return (jnp.cos(angles), jnp.sin(angles))


def swap(value, axis, mask):
    count = lax.axis_size(axis)
    return lax.ppermute(value, axis, [(i, i ^ mask) for i in range(count)])


def vmem():
    return pl.BlockSpec(memory_space=pltpu.VMEM)


def far():
    return pl.BlockSpec(memory_space=pltpu.HBM)


def smem():
    return pl.BlockSpec(memory_space=pltpu.SMEM)


def near(*arrays):
    return [pltpu.with_memory_space_constraint(a, pltpu.VMEM) for a in arrays]


def away(*arrays):
    return [pltpu.with_memory_space_constraint(a, pltpu.HBM) for a in arrays]


def room(mebibytes):
    return pltpu.CompilerParams(vmem_limit_bytes=mebibytes * 1024 * 1024)


def round_up(value, step):
    return (value + step - 1) // step * step


def dot_t(left, right):
    return lax.dot_general(
        left, right, (((1,), (1,)), ((), ())), preferred_element_type=jnp.float32
    )


def dot_exact(left, right):
    total = None
    for _ in range(3):
        part = left.astype(jnp.bfloat16)
        left = left - part.astype(jnp.float32)
        term = jnp.dot(part, right, preferred_element_type=jnp.float32)
        total = term if total is None else total + term
    return total


def fetch_kernel(order, depth, me_ref, group_ref, states_ref, *refs):
    outs, sems = refs[:-1], refs[-1]
    part_rows = outs[0].shape[0]
    start = pl.multiple_of(lax.rem(me_ref[0], 2) * part_rows, part_rows)
    copies = []
    for i, mask in enumerate(order):
        columns = pl.ds(pl.multiple_of((group_ref[0] ^ mask) * depth, LANES), depth)
        source = states_ref.at[pl.ds(start, part_rows), columns]
        copies.append(pltpu.make_async_copy(source, outs[i], sems.at[i]))
    for copy in copies:
        copy.start()
    for copy in copies:
        copy.wait()


def payload_kernel(
    layout, me_ref, blocks_ref, counts_ref, lengths_ref, keys_ref, values_ref, query_ref,
    tail_k_ref, tail_v_ref, *refs
):
    ctx_local, steps, local_heads, group_size, block_total, tail_len = layout["dims"]
    at = layout["at"]
    out_refs, sems = refs[:-1], refs[-1]
    me = me_ref[0]
    lane = lax.broadcasted_iota(jnp.int32, (NOTE_ROWS, LANES), 1)
    copies = []
    for mask, out in enumerate(out_refs):
        head = (me ^ mask) * local_heads // group_size
        columns = pl.ds(pl.multiple_of(head * HEAD_DIMENSION, HEAD_DIMENSION), HEAD_DIMENSION)
        block = jnp.clip(blocks_ref[head] - me * block_total, 0, block_total - 1)
        rows = pl.ds(pl.multiple_of(block * BLOCK_POSITIONS, BLOCK_POSITIONS), BLOCK_POSITIONS)
        moves = (
            (keys_ref.at[:, columns], 0, ctx_local),
            (values_ref.at[rows, columns], at["values"], BLOCK_POSITIONS),
            (tail_k_ref.at[:, columns], at["tail_k"], tail_len),
            (tail_v_ref.at[:, columns], at["tail_v"], tail_len),
        )
        for i, (source, start, size) in enumerate(moves):
            target = out.at[pl.ds(start, size), :]
            copies.append(pltpu.make_async_copy(source, target, sems.at[mask, i]))
            copies[-1].start()
    for mask, out in enumerate(out_refs):
        dest = me ^ mask
        head = dest * local_heads // group_size
        block = jnp.clip(blocks_ref[head] - me * block_total, 0, block_total - 1)
        parts = []
        for g in range(local_heads):
            start = (dest * local_heads + g) * HEAD_DIMENSION
            cols = pl.ds(pl.multiple_of(start, HEAD_DIMENSION), HEAD_DIMENSION)
            parts.append(query_ref[:, cols].astype(jnp.float32))
        queries = jnp.concatenate(parts, axis=0)
        pad = at["tail_k"] - at["queries"] - steps * local_heads
        if pad:
            queries = jnp.concatenate(
                [queries, jnp.zeros((pad, HEAD_DIMENSION), jnp.float32)], axis=0
            )
        out[at["queries"] : at["tail_k"], :] = queries.astype(jnp.bfloat16)
        count = counts_ref[head].astype(jnp.float32)
        notes = jnp.where(
            lane == 0,
            count,
            jnp.where(
                lane == 1,
                block.astype(jnp.float32),
                jnp.where(lane == 2, lengths_ref[0].astype(jnp.float32), 0.0),
            ),
        )
        out[at["notes"] : at["notes"] + NOTE_ROWS, :] = notes.astype(jnp.bfloat16)
    for copy in copies:
        copy.wait()


def decode_kernel(layout, me_ref, *refs):
    _, steps, local_heads, _, block_total, tail_len = layout["dims"]
    at = layout["at"]
    scale = layout["scale"]
    pieces, out_ref = refs[:-1], refs[-1]
    me = me_ref[0]
    span = steps * local_heads
    kept_k, kept_v, queries, bias, tails = [], [], [], [], []
    for piece in pieces:
        notes = piece[at["notes"] : at["notes"] + NOTE_ROWS, :].astype(jnp.float32)
        block = notes[0:1, 1:2]
        bias.append(jnp.where(notes[0:1, 0:1] > 0.5, 0.0, -1e30))
        chosen = None
        for b in range(block_total):
            cell = piece[b * BLOCK_POSITIONS : (b + 1) * BLOCK_POSITIONS, :].astype(jnp.float32)
            term = cell * jnp.where(block == float(b), 1.0, 0.0)
            chosen = term if chosen is None else chosen + term
        kept_k.append(chosen.astype(jnp.bfloat16))
        kept_v.append(piece[at["values"] : at["values"] + BLOCK_POSITIONS, :])
        own = piece[at["queries"] : at["tail_k"], :]
        if at["tail_k"] - at["queries"] > span:
            own = own.astype(jnp.float32)[:span].astype(jnp.bfloat16)
        queries.append(own)
        score = dot_t(own, piece[at["tail_k"] : at["tail_k"] + tail_len, :]) * scale
        slot = lax.broadcasted_iota(jnp.int32, (span, tail_len), 1)
        step = lax.rem(lax.broadcasted_iota(jnp.int32, (span, tail_len), 0), steps)
        visible = (slot - step).astype(jnp.float32) < notes[0:1, 2:3]
        tails.append(jnp.where(visible, score, -1e30))
    every = jnp.concatenate(queries, axis=0)
    scores = [dot_t(every, k) * scale + b for k, b in zip(kept_k, bias)]
    peak = scores[0]
    for s in scores[1:]:
        peak = jnp.maximum(peak, s)
    peak = jnp.max(peak, axis=1, keepdims=True)
    tail_peak = jnp.concatenate([jnp.max(t, axis=1, keepdims=True) for t in tails], axis=0)
    peak = jnp.maximum(peak, tail_peak)
    weights = [jnp.exp(s - peak) for s in scores]
    total = weights[0]
    for w in weights[1:]:
        total = total + w
    total = jnp.sum(total, axis=1, keepdims=True)
    numerator = dot_exact(jnp.concatenate(weights, axis=1), jnp.concatenate(kept_v, axis=0))
    for mask, piece in enumerate(pieces):
        lo = mask * span
        weight = jnp.exp(tails[mask] - peak[lo : lo + span])
        part = dot_exact(weight, piece[at["tail_v"] : at["tail_v"] + tail_len, :])
        top = numerator[lo : lo + span] + part
        bottom = total[lo : lo + span] + jnp.sum(weight, axis=1, keepdims=True)
        result = top / bottom
        dest = me ^ mask
        for g in range(local_heads):
            out_ref[dest, :, g * HEAD_DIMENSION : (g + 1) * HEAD_DIMENSION] = result[
                g * steps : (g + 1) * steps
            ].astype(jnp.bfloat16)


def votes_kernel(layout, me_ref, projected_ref, cos_ref, sin_ref, *refs):
    ctx_local, _, local_heads, group_size, _, _ = layout["dims"]
    count = layout["ctx"]
    win = projected_ref.shape[0]
    pieces, out_ref = refs[:count], refs[count + 1]
    query_ref, score_ref, peak_ref, sums_ref = refs[count + 2 :]
    me = me_ref[0]
    total_ctx = ctx_local * count
    start_pos = total_ctx - win
    folded = layout["scale"] * math.log2(math.e)
    rows = win * local_heads
    width = 2 * LANES
    half = HEAD_DIMENSION // 2
    for g in range(local_heads):
        x = projected_ref[:, g * HEAD_DIMENSION : (g + 1) * HEAD_DIMENSION]
        turned = jnp.concatenate([x[:, half:], x[:, :half]], axis=1)
        turned = x * cos_ref[...] + turned * sin_ref[...]
        query_ref[g * win : (g + 1) * win, :] = turned.astype(jnp.bfloat16)
    offset = lax.broadcasted_iota(jnp.int32, (win, LANES), 1) - lax.broadcasted_iota(
        jnp.int32, (win, LANES), 0
    )
    for mask, piece in enumerate(pieces):
        base = (me ^ mask) * ctx_local
        for c in range(0, ctx_local, width):
            score = dot_t(query_ref[...], piece[c : c + width, :])
            if c + width == ctx_local:
                seen = offset <= start_pos - base - (ctx_local - LANES)
                last = score[:, LANES:].reshape(local_heads, win, LANES)
                last = jnp.where(seen[None], last, -1e30).reshape(rows, LANES)
                score = jnp.concatenate([score[:, :LANES], last], axis=1)
            score_ref[:, pl.ds(pl.multiple_of(base + c, LANES), width)] = score
            top = jnp.maximum(score[:, :LANES], score[:, LANES:])
            first = mask == 0 and c == 0
            peak_ref[...] = top if first else jnp.maximum(peak_ref[...], top)
    votes = None
    for g in range(local_heads):
        at = slice(g * win, (g + 1) * win)
        peak = jnp.max(peak_ref[at, :], axis=1, keepdims=True) * folded
        weight = jnp.exp2(score_ref[at, :] * folded - peak)
        share = 1.0 / jnp.sum(weight, axis=1, keepdims=True)
        weight = weight * share
        cells = jnp.sum(weight.reshape(win // 8, 8, total_ctx), axis=0)
        votes = cells if votes is None else votes + cells
    row = jnp.sum(votes, axis=0, keepdims=True) * (total_ctx / (win * group_size))
    sums_ref[:, 0:LANES] = jnp.zeros((1, LANES), jnp.float32)
    sums_ref[:, LANES : LANES + total_ctx] = row
    sums_ref[:, LANES + total_ctx :] = jnp.zeros((1, LANES), jnp.float32)
    pooled = None
    for shift in range(POOL):
        start = LANES - (POOL - 1) // 2 + shift
        term = sums_ref[:, start : start + total_ctx]
        pooled = term if pooled is None else pooled + term
    pooled = pooled / POOL
    for c in range(count):
        out_ref[c] = pooled[:, c * ctx_local : (c + 1) * ctx_local]


def on_device(
    window_states,
    query_weight,
    cache_keys,
    cache_values,
    kept_blocks,
    retained_block_count,
    decode_queries,
    tail_keys,
    tail_values,
    row_lengths,
):
    ctx_count = lax.axis_size("ctx")
    grp_count = lax.axis_size("grp")
    ctx_index = lax.axis_index("ctx")
    grp_index = lax.axis_index("grp")
    states = window_states[0]
    win_rows = states.shape[0]
    depth, local_cols = query_weight.shape
    local_heads = local_cols // HEAD_DIMENSION
    head_total = local_heads * ctx_count
    group_size = head_total // KEY_HEADS
    sharers = group_size // local_heads
    ctx_local = cache_keys.shape[1]
    total_ctx = ctx_local * ctx_count
    steps = decode_queries.shape[1]
    tail_len = tail_keys.shape[2]
    block_total = ctx_local // BLOCK_POSITIONS
    assert decode_queries.shape[2] == 1 and kept_blocks.shape[2] == 1
    at, row = {}, ctx_local
    sizes = (
        ("values", BLOCK_POSITIONS),
        ("queries", round_up(steps * local_heads, 16)),
        ("tail_k", tail_len),
        ("tail_v", tail_len),
        ("notes", NOTE_ROWS),
    )
    for name, size in sizes:
        at[name] = row
        row += size
    layout = {
        "dims": (ctx_local, steps, local_heads, group_size, block_total, tail_len),
        "at": at,
        "scale": 1.0 / math.sqrt(HEAD_DIMENSION),
        "ctx": ctx_count,
    }
    me = ctx_index.astype(jnp.int32).reshape(1)
    group = grp_index.astype(jnp.int32).reshape(1)

    part_rows = win_rows // 2
    core = ctx_index % 2
    order = list(range(grp_count - 1, 0, -1))
    slices = pl.pallas_call(
        functools.partial(fetch_kernel, order, depth),
        out_shape=[pltpu.VMEM((part_rows, depth), jnp.bfloat16)] * len(order),
        in_specs=[smem(), smem(), far()],
        out_specs=[vmem()] * len(order),
        scratch_shapes=[pltpu.SemaphoreType.DMA((len(order),))],
        compiler_params=room(4),
    )(me, group, *away(states))
    fetched = {mask: swap(cell, "grp", mask) for mask, cell in zip(order, slices)}

    payload = pl.pallas_call(
        functools.partial(payload_kernel, layout),
        out_shape=[pltpu.VMEM((row, HEAD_DIMENSION), jnp.bfloat16)] * ctx_count,
        in_specs=[smem()] * 4 + [far()] * 2 + [vmem()] + [far()] * 2,
        out_specs=[vmem()] * ctx_count,
        scratch_shapes=[pltpu.SemaphoreType.DMA((ctx_count, 4))],
        compiler_params=room(8),
    )(
        me,
        kept_blocks.reshape(KEY_HEADS),
        retained_block_count.reshape(KEY_HEADS),
        row_lengths.reshape(1),
        *away(
            cache_keys[0],
            cache_values[0],
            decode_queries.reshape(steps, head_total * HEAD_DIMENSION),
            tail_keys[0, 0],
            tail_values[0, 0],
        ),
    )
    pieces = [payload[0]] + [swap(payload[m], "ctx", m) for m in range(1, ctx_count)]

    backs = []
    for mask in range(1, grp_count):
        mine = fetched[mask]
        other = swap(mine, "ctx", 1)
        both = jnp.where(
            core == 0,
            jnp.concatenate([mine, other], axis=0),
            jnp.concatenate([other, mine], axis=0),
        )
        partial = jnp.dot(both, query_weight, preferred_element_type=jnp.float32)
        backs.append(swap(partial.astype(jnp.float16), "grp", mask))
    own = lax.dynamic_slice(states, (0, grp_index * depth), (win_rows, depth))
    own, _ = lax.optimization_barrier((own, both))
    projected = jnp.dot(own, query_weight, preferred_element_type=jnp.float32)
    for back in backs:
        projected = projected + back.astype(jnp.float32)

    decoded = pl.pallas_call(
        functools.partial(decode_kernel, layout),
        out_shape=jax.ShapeDtypeStruct((ctx_count, steps, local_cols), jnp.bfloat16),
        in_specs=[smem()] + [vmem()] * ctx_count,
        out_specs=vmem(),
        compiler_params=room(8 + 24 * total_ctx // 16384),
    )(me, *near(*pieces))
    decoded = lax.all_to_all(decoded, "ctx", split_axis=0, concat_axis=0, tiled=True)
    decoded = decoded.transpose(1, 0, 2).reshape(steps, head_total * HEAD_DIMENSION)
    decode_out = decoded.reshape(1, steps, 1, head_total * HEAD_DIMENSION)

    positions = (jnp.arange(win_rows) + (total_ctx - win_rows)).astype(jnp.float32)
    cosine, sine = rotary_table(positions, HEAD_DIMENSION)
    cosine = jnp.concatenate([cosine, cosine], axis=1)
    sine = jnp.concatenate([-sine, sine], axis=1)
    pooled = pl.pallas_call(
        functools.partial(votes_kernel, layout),
        out_shape=jax.ShapeDtypeStruct((ctx_count, 1, ctx_local), jnp.float32),
        in_specs=[smem()] + [vmem()] * (3 + ctx_count) + [far()],
        out_specs=vmem(),
        compiler_params=room(20),
        scratch_shapes=[
            pltpu.VMEM((win_rows * local_heads, HEAD_DIMENSION), jnp.bfloat16),
            pltpu.VMEM((win_rows * local_heads, total_ctx), jnp.float32),
            pltpu.VMEM((win_rows * local_heads, LANES), jnp.float32),
            pltpu.VMEM((1, total_ctx + 2 * LANES), jnp.float32),
        ],
    )(me, *near(projected, cosine, sine, *pieces), *away(decoded))
    shares = lax.all_to_all(pooled, "ctx", split_axis=0, concat_axis=0, tiled=True)
    shares = shares.reshape(KEY_HEADS, sharers, ctx_local)
    pooled_votes = (shares[:, 0] if sharers == 1 else jnp.sum(shares, axis=1))[None]
    return (pooled_votes, decode_out)


def solution(mesh):
    placed = (
        P("grp", None, None),
        P("grp", "ctx"),
        P("grp", "ctx", None),
        P("grp", "ctx", None),
        P("grp", None, "ctx"),
        P("grp", None, "ctx"),
        P("grp", None, "ctx", None),
        P("grp", "ctx", None, None),
        P("grp", "ctx", None, None),
        P("grp", "ctx"),
    )

    return jax.shard_map(
        on_device,
        mesh=mesh,
        in_specs=placed,
        out_specs=(P("grp", None, "ctx"), P("grp", None, "ctx", None)),
        check_vma=False,
    )
```

profile of v0, /device:TPU:0, one launch (start us, length us, event | category | flops | bytes accessed | tf_op | source)
XLA Modules:
  0.0 76.9 jit_solution(8856770250643937408)
XLA Ops:
  0.6 1.1 %shard_map.113 = (bf16[32,2048]{1,0:T(8,128)(2,1)S(1)}, bf16[32,2048]{1,0:T(8,128)(2,1)S(1)}, bf16[32,2048]{1,0:T(8,128)(2,1)S(1)}) custom-call(s32[1]{0:T(128)} %bitcast.me_ref, s32[1]{0:T(128)} %bitcast.2.group_ref, bf16[64,8192]{1,0:T(8,128)(2,1)} %bitcast.28), custom_call_target="tpu_custom_call" | custom-call | tf_op jit(solution)/shard_map/pallas_call | solution.py:318
  1.7 3.1 %collective-permute-start.2 = (bf16[32,2048]{1,0:T(8,128)(2,1)S(1)}, bf16[32,2048]{1,0:T(8,128)(2,1)S(1)}, u32[]{:S(2)}, u32[]{:S(2)}) collective-permute-start(bf16[32,2048]{1,0:T(8,128)(2,1)S(1)} %get-tuple-element.16), channel_id=1, source_target_pairs={{0,1},{1,0},{2,3},{3,2},{4,5},{5,4},{6,7},{7,6},{8,9},{9,8},{10,11... | collective-permute-start | bytes 393224 | tf_op jit(solution)/shard_map/ppermute | solution.py:35
  4.8 2.6 %collective-permute-start.5 = (bf16[32,2048]{1,0:T(8,128)(2,1)S(1)}, bf16[32,2048]{1,0:T(8,128)(2,1)S(1)}, u32[]{:S(2)}, u32[]{:S(2)}) collective-permute-start(bf16[32,2048]{1,0:T(8,128)(2,1)S(1)} %get-tuple-element.17), channel_id=1, source_target_pairs={{0,2},{1,3},{2,0},{3,1},{4,6},{5,7},{6,4},{7,5},{8,10},{9,11},{10,... | collective-permute-start | bytes 393224 | tf_op jit(solution)/shard_map/ppermute | solution.py:35
  8.1 0.6 copy-done
  8.7 0.7 copy-done.1
  9.4 2.7 %shard_map.114 = (bf16[816,128]{1,0:T(8,128)(2,1)S(1)}, bf16[816,128]{1,0:T(8,128)(2,1)S(1)}, bf16[816,128]{1,0:T(8,128)(2,1)S(1)}, bf16[816,128]{1,0:T(8,128)(2...) custom-call(s32[1]{0:T(128)} %bitcast.me_ref, ...), custom_call_target="tpu_custom_call" | custom-call | tf_op jit(solution)/shard_map/pallas_call | solution.py:328
  12.0 1.8 %collective-permute-start.10 = (bf16[816,128]{1,0:T(8,128)(2,1)S(1)}, bf16[816,128]{1,0:T(8,128)(2,1)S(1)}, u32[]{:S(2)}, u32[]{:S(2)}) collective-permute-start(bf16[816,128]{1,0:T(8,128)(2,1)S(1)} %get-tuple-element.20), channel_id=1, source_target_pairs={{0,8},{4,12},{8,0},{12,4},{16,24},{20,28},{24,16},{28,20},{1,9},{5... | collective-permute-start | bytes 626696 | tf_op jit(solution)/shard_map/ppermute | solution.py:35
  13.8 1.0 %dynamic-slice_bitcast_fusion = bf16[64,2048]{1,0:T(8,128)(2,1)S(1)} fusion(bf16[1,64,8192]{2,1,0:T(8,128)(2,1)} %param.10, s32[]{:T(128)S(6)} %select_n.53), kind=kLoop, calls=%fused_computation.17 | loop fusion | bytes 524292 | tf_op jit(solution)/shard_map/dynamic_slice | solution.py:361
  14.8 1.6 %collective-permute-start.12 = (bf16[816,128]{1,0:T(8,128)(2,1)S(1)}, bf16[816,128]{1,0:T(8,128)(2,1)S(1)}, u32[]{:S(2)}, u32[]{:S(2)}) collective-permute-start(bf16[816,128]{1,0:T(8,128)(2,1)S(1)} %get-tuple-element.22), channel_id=1, source_target_pairs={{0,16},{4,20},{8,24},{12,28},{16,0},{20,4},{24,8},{28,12},{1,17},{... | collective-permute-start | bytes 626696 | tf_op jit(solution)/shard_map/ppermute | solution.py:35
  16.4 1.3 %collective-permute-done.5 = bf16[32,2048]{1,0:T(8,128)(2,1)S(1)} collective-permute-done((bf16[32,2048]{1,0:T(8,128)(2,1)S(1)}, bf16[32,2048]{1,0:T(8,128)(2,1)S(1)}, u32[]{:S(2)}, u32[]{:S(2)}) %collective-permute-start.5) | collective-permute-done | bytes 131104 | tf_op jit(solution)/shard_map/ppermute | solution.py:35
  17.7 2.5 %collective-permute-start.14 = (bf16[816,128]{1,0:T(8,128)(2,1)S(1)}, bf16[816,128]{1,0:T(8,128)(2,1)S(1)}, u32[]{:S(2)}, u32[]{:S(2)}) collective-permute-start(bf16[816,128]{1,0:T(8,128)(2,1)S(1)} %get-tuple-element.24), channel_id=1, source_target_pairs={{0,24},{4,28},{8,16},{12,20},{16,8},{20,12},{24,0},{28,4},{1,25},{... | collective-permute-start | bytes 626696 | tf_op jit(solution)/shard_map/ppermute | solution.py:35
  20.2 1.4 %collective-permute-start.15 = (bf16[816,128]{1,0:T(8,128)(2,1)S(1)}, bf16[816,128]{1,0:T(8,128)(2,1)S(1)}, u32[]{:S(2)}, u32[]{:S(2)}) collective-permute-start(bf16[816,128]{1,0:T(8,128)(2,1)S(1)} %get-tuple-element.25), channel_id=1, source_target_pairs={{0,28},{4,24},{8,20},{12,16},{16,12},{20,8},{24,4},{28,0},{1,29},{... | collective-permute-start | bytes 626696 | tf_op jit(solution)/shard_map/ppermute | solution.py:35
  21.6 1.4 %collective-permute-done.11.refs_3_ = bf16[816,128]{1,0:T(8,128)(2,1)S(1)} collective-permute-done((bf16[816,128]{1,0:T(8,128)(2,1)S(1)}, bf16[816,128]{1,0:T(8,128)(2,1)S(1)}, u32[]{:S(2)}, u32[]{:S(2)}) %collective-permute-start.11) | collective-permute-done | bytes 208928 | tf_op jit(solution)/shard_map/ppermute | solution.py:35
  23.0 1.1 %collective-permute-start.9 = (bf16[816,128]{1,0:T(8,128)(2,1)S(1)}, bf16[816,128]{1,0:T(8,128)(2,1)S(1)}, u32[]{:S(2)}, u32[]{:S(2)}) collective-permute-start(bf16[816,128]{1,0:T(8,128)(2,1)S(1)} %get-tuple-element.19), channel_id=1, source_target_pairs={{0,4},{4,0},{8,12},{12,8},{16,20},{20,16},{24,28},{28,24},{1,5},{5... | collective-permute-start | bytes 626696 | tf_op jit(solution)/shard_map/ppermute | solution.py:35
  24.4 10.9 %collective-permute-done.13.refs_5_ = bf16[816,128]{1,0:T(8,128)(2,1)S(1)} collective-permute-done((bf16[816,128]{1,0:T(8,128)(2,1)S(1)}, bf16[816,128]{1,0:T(8,128)(2,1)S(1)}, u32[]{:S(2)}, u32[]{:S(2)}) %collective-permute-start.13) | collective-permute-done | bytes 208928 | tf_op jit(solution)/shard_map/ppermute | solution.py:35
  35.3 0.4 collective-permute-start.6
  35.8 2.2 %shard_map.115 = bf16[8,4,1024]{2,1,0:T(4,128)(2,1)} custom-call(s32[1]{0:T(128)} %bitcast.me_ref, bf16[816,128]{1,0:T(8,128)(2,1)S(1)} %get-tuple-element.18.refs_0_, bf16[816,128]{1,0:T(8,128)(2,1)S(1)} %collective-permute-done.9.refs_1_, bf16[816,128]{1,0:T(8,128)(2,1)S(1)} %collective-permute-done.10.refs_2_, ...), custom_call_target="tpu_custom_call" | custom-call | tf_op jit(solution)/shard_map/pallas_call | solution.py:367
  38.0 3.9 %all-to-all-start = ((bf16[8,4,1024]{2,1,0:T(4,128)(2,1)}), bf16[8,4,1024]{2,1,0:T(4,128)(2,1)S(1)}, u32[]{:S(2)}, u32[]{:S(2)}) async-start(bf16[8,4,1024]{2,1,0:T(4,128)(2,1)} %shard_map.115), calls=%async_computation | async-start | bytes 131072 | tf_op jit(solution)/shard_map/all_to_all | solution.py:374
  41.8 3.3 %convolution_convert_fusion.2 = f16[64,1024]{1,0:T(8,128)(2,1)S(1)} fusion(bf16[2048,1024]{1,0:T(8,128)(2,1)} %param.11, bf16[32,2048]{1,0:T(8,128)(2,1)S(1)} %collective-permute-done.3, bf16[32,2048]{1,0:T(8,128)(2,1)} %copy-done.4, pred[]{:T(512)S(6)} %eq.4), kind=kOutput, calls=%fused_computation.2 | convolution fusion | flops 269680640 | bytes 4587521 | tf_op jit(solution)/shard_map/dot_general | solution.py:359
  45.2 0.7 collective-permute-start.4
  45.9 0.9 %convolution_convert_fusion.1 = f16[64,1024]{1,0:T(8,128)(2,1)S(1)} fusion(bf16[2048,1024]{1,0:T(8,128)(2,1)S(1)} %copy-done.2, bf16[32,2048]{1,0:T(8,128)(2,1)S(1)} %collective-permute-done.6, bf16[32,2048]{1,0:T(8,128)(2,1)S(1)} %collective-permute-done.5, pred[]{:T(512)S(6)} %eq.4), kind=kOutput, calls=%fused_computation.1 | convolution fusion | flops 269680640 | bytes 4587521 | tf_op jit(solution)/shard_map/dot_general | solution.py:359
  46.8 3.6 %collective-permute-start.7 = (f16[64,1024]{1,0:T(8,128)(2,1)S(1)}, f16[64,1024]{1,0:T(8,128)(2,1)S(1)}, u32[]{:S(2)}, u32[]{:S(2)}) collective-permute-start(f16[64,1024]{1,0:T(8,128)(2,1)S(1)} %convolution_convert_fusion.1), channel_id=1, source_target_pairs={{0,2},{1,3},{2,0},{3,1},{4,6},{5,7},{6,4},{7,5},{8,10},{9,11},{10,... | collective-permute-start | bytes 393224 | tf_op jit(solution)/shard_map/ppermute | solution.py:35
  50.4 0.8 %convolution_convert_fusion = f16[64,1024]{1,0:T(8,128)(2,1)S(1)} fusion(bf16[64,2048]{1,0:T(8,128)(2,1)S(1)} %maximum_select_fusion, bf16[2048,1024]{1,0:T(8,128)(2,1)S(1)} %copy-done.2), kind=kOutput, calls=%fused_computation | convolution fusion | flops 268500992 | bytes 4587520 | tf_op jit(solution)/shard_map/dot_general | solution.py:359
  51.2 0.3 collective-permute-start.8
  51.5 0.8 %fusion.15 = f32[64,1024]{1,0:T(8,128)S(1)} fusion(bf16[64,2048]{1,0:T(8,128)(2,1)S(1)} %dynamic-slice_bitcast_fusion, bf16[2048,1024]{1,0:T(8,128)(2,1)S(1)} %copy-done.2), kind=kOutput, calls=%fused_computation.30 | convolution fusion | flops 268435456 | bytes 4718592 | tf_op jit(solution)/shard_map/dot_general | solution.py:363
  52.4 7.9 %collective-permute-done.7 = f16[64,1024]{1,0:T(8,128)(2,1)S(1)} collective-permute-done((f16[64,1024]{1,0:T(8,128)(2,1)S(1)}, f16[64,1024]{1,0:T(8,128)(2,1)S(1)}, u32[]{:S(2)}, u32[]{:S(2)}) %collective-permute-start.7) | collective-permute-done | bytes 131104 | tf_op jit(solution)/shard_map/ppermute | solution.py:35
  60.4 0.6 copy-done.3
  61.0 4.8 %shard_map.116 = f32[8,1,512]{2,1,0:T(1,128)} custom-call(s32[1]{0:T(128)} %bitcast.me_ref, f32[64,1024]{1,0:T(8,128)S(1)} %convert_add_fusion.projected_ref, f32[64,128]{1,0:T(8,128)S(1)} %get-tuple-element.31.cos_ref, f32[64,128]{1,0:T(8,128)S(1)} %get-tuple-element.32.sin_ref, bf16[816,128]{1,0:T(8,128)(2,1)S(1)} %get-tuple-element.18.refs_0_, ...), custom_call_target="tpu_custom_call" | custom-call | tf_op jit(solution)/shard_map/pallas_call | solution.py:382
  65.8 4.2 %all-to-all-start.1 = ((f32[8,1,512]{2,1,0:T(1,128)}), f32[8,1,512]{2,1,0:T(1,128)S(1)}, u32[]{:S(2)}, u32[]{:S(2)}) async-start(f32[8,1,512]{2,1,0:T(1,128)} %shard_map.116), calls=%async_computation.1 | async-start | bytes 32768 | tf_op jit(solution)/shard_map/all_to_all | solution.py:395
  70.0 4.8 %all-to-all-done.1 = f32[8,1,512]{2,1,0:T(1,128)S(1)} async-done(((f32[8,1,512]{2,1,0:T(1,128)}), f32[8,1,512]{2,1,0:T(1,128)S(1)}, u32[]{:S(2)}, u32[]{:S(2)}) %all-to-all-start.1) | async-done | bytes 16416 | tf_op jit(solution)/shard_map/all_to_all | solution.py:395
  74.8 0.6 copy.12
  75.4 1.5 %copy.15 = bf16[1,4,1,8192]{3,1,2,0:T(4,128)(2,1)} copy(bf16[1,4,1,8192]{3,1,2,0:T(4,128)(2,1)} %bitcast.32) | data formatting | bytes 131072
  (31 shorter events, 0.6 us)
Async XLA Ops:
  1.7 13.1 %collective-permute-start.2 = (bf16[32,2048]{1,0:T(8,128)(2,1)S(1)}, bf16[32,2048]{1,0:T(8,128)(2,1)S(1)}, u32[]{:S(2)}, u32[]{:S(2)}) collective-permute-start(bf16[32,2048]{1,0:T(8,128)(2,1)S(1)} %get-tuple-element.16), channel_id=1, source_target_pairs={{0,1},{1,0},{2,3},{3,2},{4,5},{5,4},{6,7},{7,6},{8,9},{9,8},{10,11... | collective-permute-start | bytes 393224 | tf_op jit(solution)/shard_map/ppermute | solution.py:35
  4.8 12.9 %collective-permute-start.5 = (bf16[32,2048]{1,0:T(8,128)(2,1)S(1)}, bf16[32,2048]{1,0:T(8,128)(2,1)S(1)}, u32[]{:S(2)}, u32[]{:S(2)}) collective-permute-start(bf16[32,2048]{1,0:T(8,128)(2,1)S(1)} %get-tuple-element.17), channel_id=1, source_target_pairs={{0,2},{1,3},{2,0},{3,1},{4,6},{5,7},{6,4},{7,5},{8,10},{9,11},{10,... | collective-permute-start | bytes 393224 | tf_op jit(solution)/shard_map/ppermute | solution.py:35
  7.4 10.3 %collective-permute-start = (bf16[32,2048]{1,0:T(8,128)(2,1)S(1)}, bf16[32,2048]{1,0:T(8,128)(2,1)S(1)}, u32[]{:S(2)}, u32[]{:S(2)}) collective-permute-start(bf16[32,2048]{1,0:T(8,128)(2,1)S(1)} %get-tuple-element.14), channel_id=1, source_target_pairs={{0,3},{1,2},{2,1},{3,0},{4,7},{5,6},{6,5},{7,4},{8,11},{9,10},{10,... | collective-permute-start | bytes 393224 | tf_op jit(solution)/shard_map/ppermute | solution.py:35
  8.1 0.7 copy-start
  8.7 0.7 copy-start.1
  12.0 8.2 %collective-permute-start.10 = (bf16[816,128]{1,0:T(8,128)(2,1)S(1)}, bf16[816,128]{1,0:T(8,128)(2,1)S(1)}, u32[]{:S(2)}, u32[]{:S(2)}) collective-permute-start(bf16[816,128]{1,0:T(8,128)(2,1)S(1)} %get-tuple-element.20), channel_id=1, source_target_pairs={{0,8},{4,12},{8,0},{12,4},{16,24},{20,28},{24,16},{28,20},{1,9},{5... | collective-permute-start | bytes 626696 | tf_op jit(solution)/shard_map/ppermute | solution.py:35
  13.8 9.2 %collective-permute-start.11 = (bf16[816,128]{1,0:T(8,128)(2,1)S(1)}, bf16[816,128]{1,0:T(8,128)(2,1)S(1)}, u32[]{:S(2)}, u32[]{:S(2)}) collective-permute-start(bf16[816,128]{1,0:T(8,128)(2,1)S(1)} %get-tuple-element.21), channel_id=1, source_target_pairs={{0,12},{4,8},{8,4},{12,0},{16,28},{20,24},{24,20},{28,16},{1,13},{... | collective-permute-start | bytes 626696 | tf_op jit(solution)/shard_map/ppermute | solution.py:35
  14.8 2.9 %copy-start.4 = (bf16[32,2048]{1,0:T(8,128)(2,1)}, bf16[32,2048]{1,0:T(8,128)(2,1)S(1)}, u32[]{:S(2)}) copy-start(bf16[32,2048]{1,0:T(8,128)(2,1)S(1)} %collective-permute-done.2) | copy-start | bytes 393220
  14.8 9.3 %collective-permute-start.12 = (bf16[816,128]{1,0:T(8,128)(2,1)S(1)}, bf16[816,128]{1,0:T(8,128)(2,1)S(1)}, u32[]{:S(2)}, u32[]{:S(2)}) collective-permute-start(bf16[816,128]{1,0:T(8,128)(2,1)S(1)} %get-tuple-element.22), channel_id=1, source_target_pairs={{0,16},{4,20},{8,24},{12,28},{16,0},{20,4},{24,8},{28,12},{1,17},{... | collective-permute-start | bytes 626696 | tf_op jit(solution)/shard_map/ppermute | solution.py:35
  17.7 17.6 %collective-permute-start.13 = (bf16[816,128]{1,0:T(8,128)(2,1)S(1)}, bf16[816,128]{1,0:T(8,128)(2,1)S(1)}, u32[]{:S(2)}, u32[]{:S(2)}) collective-permute-start(bf16[816,128]{1,0:T(8,128)(2,1)S(1)} %get-tuple-element.23), channel_id=1, source_target_pairs={{0,20},{4,16},{8,28},{12,24},{16,4},{20,0},{24,12},{28,8},{1,21},{... | collective-permute-start | bytes 626696 | tf_op jit(solution)/shard_map/ppermute | solution.py:35
  17.7 17.9 %collective-permute-start.14 = (bf16[816,128]{1,0:T(8,128)(2,1)S(1)}, bf16[816,128]{1,0:T(8,128)(2,1)S(1)}, u32[]{:S(2)}, u32[]{:S(2)}) collective-permute-start(bf16[816,128]{1,0:T(8,128)(2,1)S(1)} %get-tuple-element.24), channel_id=1, source_target_pairs={{0,24},{4,28},{8,16},{12,20},{16,8},{20,12},{24,0},{28,4},{1,25},{... | collective-permute-start | bytes 626696 | tf_op jit(solution)/shard_map/ppermute | solution.py:35
  20.2 15.5 %collective-permute-start.15 = (bf16[816,128]{1,0:T(8,128)(2,1)S(1)}, bf16[816,128]{1,0:T(8,128)(2,1)S(1)}, u32[]{:S(2)}, u32[]{:S(2)}) collective-permute-start(bf16[816,128]{1,0:T(8,128)(2,1)S(1)} %get-tuple-element.25), channel_id=1, source_target_pairs={{0,28},{4,24},{8,20},{12,16},{16,12},{20,8},{24,4},{28,0},{1,29},{... | collective-permute-start | bytes 626696 | tf_op jit(solution)/shard_map/ppermute | solution.py:35
  23.0 12.8 %collective-permute-start.9 = (bf16[816,128]{1,0:T(8,128)(2,1)S(1)}, bf16[816,128]{1,0:T(8,128)(2,1)S(1)}, u32[]{:S(2)}, u32[]{:S(2)}) collective-permute-start(bf16[816,128]{1,0:T(8,128)(2,1)S(1)} %get-tuple-element.19), channel_id=1, source_target_pairs={{0,4},{4,0},{8,12},{12,8},{16,20},{20,16},{24,28},{28,24},{1,5},{5... | collective-permute-start | bytes 626696 | tf_op jit(solution)/shard_map/ppermute | solution.py:35
  24.1 17.7 %collective-permute-start.3 = (bf16[32,2048]{1,0:T(8,128)(2,1)}, bf16[32,2048]{1,0:T(8,128)(2,1)S(1)}, u32[]{:S(2)}, u32[]{:S(2)}) collective-permute-start(bf16[32,2048]{1,0:T(8,128)(2,1)} %copy-done.4), channel_id=1, source_target_pairs={{0,4},{4,0},{8,12},{12,8},{16,20},{20,16},{24,28},{28,24},{1,5},{5... | collective-permute-start | bytes 393224 | tf_op jit(solution)/shard_map/ppermute | solution.py:35
  35.3 10.6 %collective-permute-start.6 = (bf16[32,2048]{1,0:T(8,128)(2,1)S(1)}, bf16[32,2048]{1,0:T(8,128)(2,1)S(1)}, u32[]{:S(2)}, u32[]{:S(2)}) collective-permute-start(bf16[32,2048]{1,0:T(8,128)(2,1)S(1)} %collective-permute-done.5), channel_id=1, source_target_pairs={{0,4},{4,0},{8,12},{12,8},{16,20},{20,16},{24,28},{28,24},{1,5},{5... | collective-permute-start | bytes 393224 | tf_op jit(solution)/shard_map/ppermute | solution.py:35
  35.6 14.7 %collective-permute-start.1 = (bf16[32,2048]{1,0:T(8,128)(2,1)S(1)}, bf16[32,2048]{1,0:T(8,128)(2,1)S(1)}, u32[]{:S(2)}, u32[]{:S(2)}) collective-permute-start(bf16[32,2048]{1,0:T(8,128)(2,1)S(1)} %collective-permute-done), channel_id=1, source_target_pairs={{0,4},{4,0},{8,12},{12,8},{16,20},{20,16},{24,28},{28,24},{1,5},{5... | collective-permute-start | bytes 393224 | tf_op jit(solution)/shard_map/ppermute | solution.py:35
  38.0 22.4 %all-to-all-start = ((bf16[8,4,1024]{2,1,0:T(4,128)(2,1)}), bf16[8,4,1024]{2,1,0:T(4,128)(2,1)S(1)}, u32[]{:S(2)}, u32[]{:S(2)}) async-start(bf16[8,4,1024]{2,1,0:T(4,128)(2,1)} %shard_map.115), calls=%async_computation | async-start | bytes 131072 | tf_op jit(solution)/shard_map/all_to_all | solution.py:374
  41.8 4.1 %copy-start.2 = (bf16[2048,1024]{1,0:T(8,128)(2,1)S(1)}, bf16[2048,1024]{1,0:T(8,128)(2,1)}, u32[]{:S(2)}) copy-start(bf16[2048,1024]{1,0:T(8,128)(2,1)} %param.11) | copy-start | bytes 12582916
  45.2 7.2 %collective-permute-start.4 = (f16[64,1024]{1,0:T(8,128)(2,1)S(1)}, f16[64,1024]{1,0:T(8,128)(2,1)S(1)}, u32[]{:S(2)}, u32[]{:S(2)}) collective-permute-start(f16[64,1024]{1,0:T(8,128)(2,1)S(1)} %convolution_convert_fusion.2), channel_id=1, source_target_pairs={{0,1},{1,0},{2,3},{3,2},{4,5},{5,4},{6,7},{7,6},{8,9},{9,8},{10,11... | collective-permute-start | bytes 393224 | tf_op jit(solution)/shard_map/ppermute | solution.py:35
  46.8 13.5 %collective-permute-start.7 = (f16[64,1024]{1,0:T(8,128)(2,1)S(1)}, f16[64,1024]{1,0:T(8,128)(2,1)S(1)}, u32[]{:S(2)}, u32[]{:S(2)}) collective-permute-start(f16[64,1024]{1,0:T(8,128)(2,1)S(1)} %convolution_convert_fusion.1), channel_id=1, source_target_pairs={{0,2},{1,3},{2,0},{3,1},{4,6},{5,7},{6,4},{7,5},{8,10},{9,11},{10,... | collective-permute-start | bytes 393224 | tf_op jit(solution)/shard_map/ppermute | solution.py:35
  51.2 9.1 %collective-permute-start.8 = (f16[64,1024]{1,0:T(8,128)(2,1)S(1)}, f16[64,1024]{1,0:T(8,128)(2,1)S(1)}, u32[]{:S(2)}, u32[]{:S(2)}) collective-permute-start(f16[64,1024]{1,0:T(8,128)(2,1)S(1)} %convolution_convert_fusion), channel_id=1, source_target_pairs={{0,3},{1,2},{2,1},{3,0},{4,7},{5,6},{6,5},{7,4},{8,11},{9,10},{10,... | collective-permute-start | bytes 393224 | tf_op jit(solution)/shard_map/ppermute | solution.py:35
  60.4 0.6 copy-start.3
  65.8 8.9 %all-to-all-start.1 = ((f32[8,1,512]{2,1,0:T(1,128)}), f32[8,1,512]{2,1,0:T(1,128)S(1)}, u32[]{:S(2)}, u32[]{:S(2)}) async-start(f32[8,1,512]{2,1,0:T(1,128)} %shard_map.116), calls=%async_computation.1 | async-start | bytes 32768 | tf_op jit(solution)/shard_map/all_to_all | solution.py:395
where the time goes:
time: 77.3 us; the launch traced here: 76.9 us
  starting transfers between devices  27.2 us (35%)
  waiting for transfers between devices  26.2 us (34%)
  Pallas kernels  10.7 us (14%)
  matrix products  5.85 us (8%)
  local copies, waits for them, and re-layouts  4.99 us (6%)
  between operations  1.45 us (2%)
    ppermute x16, waiting for transfers between devices, swap(): return lax.ppermute(value, axis, [(i, i ^ mask) for i in range(count)])  21.5 us
    ppermute x16, starting transfers between devices, swap(): return lax.ppermute(value, axis, [(i, i ^ mask) for i in range(count)])  19.2 us
    dot_general x3, matrix products, on_device(): partial = jnp.dot(both, query_weight, preferred_element_type=jnp.float32)  5.01 us
    pallas_call x1, Pallas kernels, on_device(): pl.pallas_call(functools.partial(votes_kernel, layout), out_shape=jax.Sha...  4.8 us
    all_to_all x1, waiting for transfers between devices, on_device(): lax.all_to_all(pooled, 'ctx', split_axis=0, concat_axis=0, tiled=True)  4.75 us
    all_to_all x1, starting transfers between devices, on_device(): lax.all_to_all(pooled, 'ctx', split_axis=0, concat_axis=0, tiled=True)  4.19 us
    unnamed x12, local copies, waits for them, and re-layouts  4.03 us
    all_to_all x1, starting transfers between devices, on_device(): lax.all_to_all(decoded, 'ctx', split_axis=0, concat_axis=0, tiled=True)  3.85 us
  transfers between devices with their start and end apart: 18, of which 5 were waited for; matrix products, arithmetic and copies ran while one was open for 9% of the time, Pallas kernels for 6%

commit v1 on v0

--- a/solution.py
+++ b/solution.py
@@ -95,12 +95,12 @@
 
 
 def payload_kernel(
-    layout, me_ref, blocks_ref, counts_ref, lengths_ref, keys_ref, values_ref, query_ref,
-    tail_k_ref, tail_v_ref, *refs
+    layout, me_ref, group_ref, blocks_ref, counts_ref, lengths_ref, keys_ref, values_ref,
+    query_ref, tail_k_ref, tail_v_ref, states_ref, *refs
 ):
     ctx_local, steps, local_heads, group_size, block_total, tail_len = layout["dims"]
     at = layout["at"]
-    out_refs, sems = refs[:-1], refs[-1]
+    out_refs, own_ref, sems, own_sems = refs[:-3], refs[-3], refs[-2], refs[-1]
     me = me_ref[0]
     lane = lax.broadcasted_iota(jnp.int32, (NOTE_ROWS, LANES), 1)
     copies = []
@@ -119,6 +119,16 @@
             target = out.at[pl.ds(start, size), :]
             copies.append(pltpu.make_async_copy(source, target, sems.at[mask, i]))
             copies[-1].start()
+    win, depth = own_ref.shape
+    half = win // 2
+    columns = pl.ds(pl.multiple_of(group_ref[0] * depth, LANES), depth)
+    for i in range(2):
+        start = pl.multiple_of((lax.rem(me, 2) ^ i) * half, half)
+        source = states_ref.at[pl.ds(start, half), columns]
+        copies.append(
+            pltpu.make_async_copy(source, own_ref.at[pl.ds(i * half, half), :], own_sems.at[i])
+        )
+        copies[-1].start()
     for mask, out in enumerate(out_refs):
         dest = me ^ mask
         head = dest * local_heads // group_size
@@ -210,8 +220,8 @@
     ctx_local, _, local_heads, group_size, _, _ = layout["dims"]
     count = layout["ctx"]
     win = projected_ref.shape[0]
-    pieces, out_ref = refs[:count], refs[count + 1]
-    query_ref, score_ref, peak_ref, sums_ref = refs[count + 2 :]
+    pieces, out_ref = refs[:count], refs[count]
+    query_ref, score_ref, peak_ref, sums_ref = refs[count + 1 :]
     me = me_ref[0]
     total_ctx = ctx_local * count
     start_pos = total_ctx - win
@@ -219,14 +229,17 @@
     rows = win * local_heads
     width = 2 * LANES
     half = HEAD_DIMENSION // 2
+    parts = [pl.ds(pl.multiple_of((lax.rem(me, 2) ^ i) * (win // 2), win // 2), win // 2) for i in (0, 1)]
+    cosine = jnp.concatenate([cos_ref[part, :] for part in parts], axis=0)
+    sine = jnp.concatenate([sin_ref[part, :] for part in parts], axis=0)
     for g in range(local_heads):
         x = projected_ref[:, g * HEAD_DIMENSION : (g + 1) * HEAD_DIMENSION]
         turned = jnp.concatenate([x[:, half:], x[:, :half]], axis=1)
-        turned = x * cos_ref[...] + turned * sin_ref[...]
+        turned = x * cosine + turned * sine
         query_ref[g * win : (g + 1) * win, :] = turned.astype(jnp.bfloat16)
-    offset = lax.broadcasted_iota(jnp.int32, (win, LANES), 1) - lax.broadcasted_iota(
-        jnp.int32, (win, LANES), 0
-    )
+    window_row = lax.broadcasted_iota(jnp.int32, (win, LANES), 0) + lax.rem(me, 2) * (win // 2)
+    window_row = jnp.where(window_row >= win, window_row - win, window_row)
+    offset = lax.broadcasted_iota(jnp.int32, (win, LANES), 1) - window_row
     for mask, piece in enumerate(pieces):
         base = (me ^ mask) * ctx_local
         for c in range(0, ctx_local, width):
@@ -313,7 +326,6 @@
     group = grp_index.astype(jnp.int32).reshape(1)
 
     part_rows = win_rows // 2
-    core = ctx_index % 2
     order = list(range(grp_count - 1, 0, -1))
     slices = pl.pallas_call(
         functools.partial(fetch_kernel, order, depth),
@@ -325,17 +337,21 @@
     )(me, group, *away(states))
     fetched = {mask: swap(cell, "grp", mask) for mask, cell in zip(order, slices)}
 
-    payload = pl.pallas_call(
+    *payload, own = pl.pallas_call(
         functools.partial(payload_kernel, layout),
-        out_shape=[pltpu.VMEM((row, HEAD_DIMENSION), jnp.bfloat16)] * ctx_count,
-        in_specs=[smem()] * 4 + [far()] * 2 + [vmem()] + [far()] * 2,
-        out_specs=[vmem()] * ctx_count,
-        scratch_shapes=[pltpu.SemaphoreType.DMA((ctx_count, 4))],
+        out_shape=[pltpu.VMEM((row, HEAD_DIMENSION), jnp.bfloat16)] * ctx_count
+        + [pltpu.VMEM((win_rows, depth), jnp.bfloat16)],
+        in_specs=[smem()] * 5 + [far()] * 2 + [vmem()] + [far()] * 3,
+        out_specs=[vmem()] * (ctx_count + 1),
+        scratch_shapes=[
+            pltpu.SemaphoreType.DMA((ctx_count, 4)),
+            pltpu.SemaphoreType.DMA((2,)),
+        ],
         compiler_params=room(8),
     )(
         me,
-        kept_blocks.reshape(KEY_HEADS),
-        retained_block_count.reshape(KEY_HEADS),
+        group,
+        *away(kept_blocks.reshape(KEY_HEADS), retained_block_count.reshape(KEY_HEADS)),
         row_lengths.reshape(1),
         *away(
             cache_keys[0],
@@ -343,6 +359,7 @@
             decode_queries.reshape(steps, head_total * HEAD_DIMENSION),
             tail_keys[0, 0],
             tail_values[0, 0],
+            states,
         ),
     )
     pieces = [payload[0]] + [swap(payload[m], "ctx", m) for m in range(1, ctx_count)]
@@ -351,15 +368,9 @@
     for mask in range(1, grp_count):
         mine = fetched[mask]
         other = swap(mine, "ctx", 1)
-        both = jnp.where(
-            core == 0,
-            jnp.concatenate([mine, other], axis=0),
-            jnp.concatenate([other, mine], axis=0),
-        )
+        both = jnp.concatenate([mine, other], axis=0)
         partial = jnp.dot(both, query_weight, preferred_element_type=jnp.float32)
         backs.append(swap(partial.astype(jnp.float16), "grp", mask))
-    own = lax.dynamic_slice(states, (0, grp_index * depth), (win_rows, depth))
-    own, _ = lax.optimization_barrier((own, both))
     projected = jnp.dot(own, query_weight, preferred_element_type=jnp.float32)
     for back in backs:
         projected = projected + back.astype(jnp.float32)
@@ -382,7 +393,7 @@
     pooled = pl.pallas_call(
         functools.partial(votes_kernel, layout),
         out_shape=jax.ShapeDtypeStruct((ctx_count, 1, ctx_local), jnp.float32),
-        in_specs=[smem()] + [vmem()] * (3 + ctx_count) + [far()],
+        in_specs=[smem()] + [vmem()] * (3 + ctx_count),
         out_specs=vmem(),
         compiler_params=room(20),
         scratch_shapes=[
@@ -391,7 +402,7 @@
             pltpu.VMEM((win_rows * local_heads, LANES), jnp.float32),
             pltpu.VMEM((1, total_ctx + 2 * LANES), jnp.float32),
         ],
-    )(me, *near(projected, cosine, sine, *pieces), *away(decoded))
+    )(me, *near(projected, cosine, sine, *pieces))
     shares = lax.all_to_all(pooled, "ctx", split_axis=0, concat_axis=0, tiled=True)
     shares = shares.reshape(KEY_HEADS, sharers, ctx_local)
     pooled_votes = (shares[:, 0] if sharers == 1 else jnp.sum(shares, axis=1))[None]

time: 77.3 us -> 61.9 us (0.80)
  waiting for transfers between devices: 26.2 us -> 20.4 us
  local copies, waits for them, and re-layouts: 4.99 us -> 1.24 us
  starting transfers between devices: 27.2 us -> 23.7 us
  matrix products: 5.85 us -> 3.43 us
    ppermute x16, waiting for transfers between devices: 21.5 us -> 15.7 us  [swap(): return lax.ppermute(value, axis, [(i, i ^ mask) for i in range(count)])]
    unnamed x12 -> x4, local copies, waits for them, and re-layouts: 4.03 us -> 1.24 us
    dot_general x3, matrix products: 5.01 us -> 2.58 us  [on_device(): partial = jnp.dot(both, query_weight, preferred_element_type=jnp.float32)]
    ppermute x16, starting transfers between devices: 19.2 us -> 16.9 us  [swap(): return lax.ppermute(value, axis, [(i, i ^ mask) for i in range(count)])]
    dynamic_slice x1 -> x0, local copies, waits for them, and re-layouts: 0.97 us -> none  [on_device(): own = lax.dynamic_slice(states, (0, grp_index * depth), (win_rows, depth))]
  transfers between devices with their start and end apart: 18 -> 18, of which waited for: 5 -> 6; matrix products, arithmetic and copies ran while one was open for 9% -> 6% of each run, Pallas kernels for 6% -> 16%
where the time goes in v1:
time: 61.9 us; the launch traced here: 61.5 us
  starting transfers between devices  23.7 us (38%)
  waiting for transfers between devices  20.4 us (33%)
  Pallas kernels  11 us (18%)
  matrix products  3.43 us (6%)
  between operations  1.45 us (2%)
  local copies, waits for them, and re-layouts  1.24 us (2%)
    ppermute x16, starting transfers between devices, swap(): return lax.ppermute(value, axis, [(i, i ^ mask) for i in range(count)])  16.9 us
    ppermute x16, waiting for transfers between devices, swap(): return lax.ppermute(value, axis, [(i, i ^ mask) for i in range(count)])  15.7 us
    pallas_call x1, Pallas kernels, on_device(): pl.pallas_call(functools.partial(votes_kernel, layout), out_shape=jax.Sha...  4.76 us
    all_to_all x1, waiting for transfers between devices, on_device(): lax.all_to_all(pooled, 'ctx', split_axis=0, concat_axis=0, tiled=True)  4.75 us
    all_to_all x1, starting transfers between devices, on_device(): lax.all_to_all(pooled, 'ctx', split_axis=0, concat_axis=0, tiled=True)  3.43 us
    all_to_all x1, starting transfers between devices, on_device(): lax.all_to_all(decoded, 'ctx', split_axis=0, concat_axis=0, tiled=True)  3.35 us
    pallas_call x1, Pallas kernels, on_device(): pl.pallas_call(functools.partial(payload_kernel, layout), out_shape=[pltp...  2.8 us
    dot_general x3, matrix products, on_device(): partial = jnp.dot(both, query_weight, preferred_element_type=jnp.float32)  2.58 us
  transfers between devices with their start and end apart: 18, of which 6 were waited for; matrix products, arithmetic and copies ran while one was open for 6% of the time, Pallas kernels for 16%

profile of v1, /device:TPU:0, one launch (start us, length us, event | category | flops | bytes accessed | tf_op | source)
XLA Modules:
  0.0 61.5 jit_solution(8057030667930620195)
XLA Ops:
  0.6 1.2 %shard_map.114 = (bf16[32,2048]{1,0:T(8,128)(2,1)S(1)}, bf16[32,2048]{1,0:T(8,128)(2,1)S(1)}, bf16[32,2048]{1,0:T(8,128)(2,1)S(1)}) custom-call(s32[1]{0:T(128)} %bitcast.me_ref, s32[1]{0:T(128)} %bitcast.1.group_ref, bf16[64,8192]{1,0:T(8,128)(2,1)} %bitcast.21), custom_call_target="tpu_custom_call" | custom-call | tf_op jit(solution)/shard_map/pallas_call | solution.py:330
  1.9 5.1 %collective-permute-start.6 = (bf16[32,2048]{1,0:T(8,128)(2,1)S(1)}, bf16[32,2048]{1,0:T(8,128)(2,1)S(1)}, u32[]{:S(2)}, u32[]{:S(2)}) collective-permute-start(bf16[32,2048]{1,0:T(8,128)(2,1)S(1)} %get-tuple-element.17), channel_id=1, source_target_pairs={{0,3},{1,2},{2,1},{3,0},{4,7},{5,6},{6,5},{7,4},{8,11},{9,10},{10,... | collective-permute-start | bytes 393224 | tf_op jit(solution)/shard_map/ppermute | solution.py:35
  7.0 0.6 %collective-permute-start = (bf16[32,2048]{1,0:T(8,128)(2,1)S(1)}, bf16[32,2048]{1,0:T(8,128)(2,1)S(1)}, u32[]{:S(2)}, u32[]{:S(2)}) collective-permute-start(bf16[32,2048]{1,0:T(8,128)(2,1)S(1)} %get-tuple-element.15), channel_id=1, source_target_pairs={{0,1},{1,0},{2,3},{3,2},{4,5},{5,4},{6,7},{7,6},{8,9},{9,8},{10,11... | collective-permute-start | bytes 393224 | tf_op jit(solution)/shard_map/ppermute | solution.py:35
  8.3 2.8 %shard_map.113 = (bf16[816,128]{1,0:T(8,128)(2,1)S(1)}, bf16[816,128]{1,0:T(8,128)(2,1)S(1)}, bf16[816,128]{1,0:T(8,128)(2,1)S(1)}, bf16[816,128]{1,0:T(8,128)(2...) custom-call(s32[1]{0:T(128)} %bitcast.me_ref, ...), custom_call_target="tpu_custom_call" | custom-call | tf_op jit(solution)/shard_map/pallas_call | solution.py:340
  11.2 1.7 %collective-permute-start.10 = (bf16[816,128]{1,0:T(8,128)(2,1)S(1)}, bf16[816,128]{1,0:T(8,128)(2,1)S(1)}, u32[]{:S(2)}, u32[]{:S(2)}) collective-permute-start(bf16[816,128]{1,0:T(8,128)(2,1)S(1)} %get-tuple-element.20), channel_id=1, source_target_pairs={{0,8},{4,12},{8,0},{12,4},{16,24},{20,28},{24,16},{28,20},{1,9},{5... | collective-permute-start | bytes 626696 | tf_op jit(solution)/shard_map/ppermute | solution.py:35
  12.9 0.9 %fusion.13 = f32[64,1024]{1,0:T(8,128)S(1)} fusion(bf16[64,2048]{1,0:T(8,128)(2,1)S(1)} %get-tuple-element.14, bf16[2048,1024]{1,0:T(8,128)(2,1)S(1)} %copy-done), kind=kOutput, calls=%fused_computation.24 | convolution fusion | flops 268435456 | bytes 4718592 | tf_op jit(solution)/shard_map/dot_general | solution.py:374
  13.8 0.2 collective-permute-start.7
  14.0 4.1 %collective-permute-done.3 = bf16[32,2048]{1,0:T(8,128)(2,1)S(1)} collective-permute-done((bf16[32,2048]{1,0:T(8,128)(2,1)S(1)}, bf16[32,2048]{1,0:T(8,128)(2,1)S(1)}, u32[]{:S(2)}, u32[]{:S(2)}) %collective-permute-start.3) | collective-permute-done | bytes 131104 | tf_op jit(solution)/shard_map/ppermute | solution.py:35
  18.1 0.3 collective-permute-start.11
  18.4 1.3 %collective-permute-start.4 = (bf16[32,2048]{1,0:T(8,128)(2,1)S(1)}, bf16[32,2048]{1,0:T(8,128)(2,1)S(1)}, u32[]{:S(2)}, u32[]{:S(2)}) collective-permute-start(bf16[32,2048]{1,0:T(8,128)(2,1)S(1)} %collective-permute-done.3), channel_id=1, source_target_pairs={{0,4},{4,0},{8,12},{12,8},{16,20},{20,16},{24,28},{28,24},{1,5},{5... | collective-permute-start | bytes 393224 | tf_op jit(solution)/shard_map/ppermute | solution.py:35
  19.7 0.9 %convolution_convert_fusion = f16[64,1024]{1,0:T(8,128)(2,1)S(1)} fusion(bf16[2048,1024]{1,0:T(8,128)(2,1)S(1)} %copy-done, bf16[32,2048]{1,0:T(8,128)(2,1)S(1)} %collective-permute-done.7, bf16[32,2048]{1,0:T(8,128)(2,1)S(1)} %collective-permute-done.6), kind=kOutput, calls=%fused_computation | convolution fusion | flops 269025280 | bytes 4587520 | tf_op jit(solution)/shard_map/dot_general | solution.py:372
  20.6 1.6 %collective-permute-start.12 = (bf16[816,128]{1,0:T(8,128)(2,1)S(1)}, bf16[816,128]{1,0:T(8,128)(2,1)S(1)}, u32[]{:S(2)}, u32[]{:S(2)}) collective-permute-start(bf16[816,128]{1,0:T(8,128)(2,1)S(1)} %get-tuple-element.22), channel_id=1, source_target_pairs={{0,16},{4,20},{8,24},{12,28},{16,0},{20,4},{24,8},{28,12},{1,17},{... | collective-permute-start | bytes 626696 | tf_op jit(solution)/shard_map/ppermute | solution.py:35
  22.2 0.9 %convolution_convert_fusion.1 = f16[64,1024]{1,0:T(8,128)(2,1)S(1)} fusion(bf16[2048,1024]{1,0:T(8,128)(2,1)S(1)} %copy-done, bf16[32,2048]{1,0:T(8,128)(2,1)S(1)} %collective-permute-done.4, bf16[32,2048]{1,0:T(8,128)(2,1)S(1)} %collective-permute-done.3), kind=kOutput, calls=%fused_computation.1 | convolution fusion | flops 269025280 | bytes 4587520 | tf_op jit(solution)/shard_map/dot_general | solution.py:372
  23.0 0.5 collective-permute-done.1
  23.5 0.3 collective-permute-start.13
  23.8 0.9 %convolution_convert_fusion.2 = f16[64,1024]{1,0:T(8,128)(2,1)S(1)} fusion(bf16[2048,1024]{1,0:T(8,128)(2,1)S(1)} %copy-done, bf16[32,2048]{1,0:T(8,128)(2,1)S(1)} %collective-permute-done.1, bf16[32,2048]{1,0:T(8,128)(2,1)S(1)} %collective-permute-done), kind=kOutput, calls=%fused_computation.2 | convolution fusion | flops 269025280 | bytes 4587520 | tf_op jit(solution)/shard_map/dot_general | solution.py:372
  24.7 1.6 %collective-permute-start.14 = (bf16[816,128]{1,0:T(8,128)(2,1)S(1)}, bf16[816,128]{1,0:T(8,128)(2,1)S(1)}, u32[]{:S(2)}, u32[]{:S(2)}) collective-permute-start(bf16[816,128]{1,0:T(8,128)(2,1)S(1)} %get-tuple-element.24), channel_id=1, source_target_pairs={{0,24},{4,28},{8,16},{12,20},{16,8},{20,12},{24,0},{28,4},{1,25},{... | collective-permute-start | bytes 626696 | tf_op jit(solution)/shard_map/ppermute | solution.py:35
  26.2 1.1 %collective-permute-start.15 = (bf16[816,128]{1,0:T(8,128)(2,1)S(1)}, bf16[816,128]{1,0:T(8,128)(2,1)S(1)}, u32[]{:S(2)}, u32[]{:S(2)}) collective-permute-start(bf16[816,128]{1,0:T(8,128)(2,1)S(1)} %get-tuple-element.25), channel_id=1, source_target_pairs={{0,28},{4,24},{8,20},{12,16},{16,12},{20,8},{24,4},{28,0},{1,29},{... | collective-permute-start | bytes 626696 | tf_op jit(solution)/shard_map/ppermute | solution.py:35
  27.3 2.5 %collective-permute-start.8 = (f16[64,1024]{1,0:T(8,128)(2,1)S(1)}, f16[64,1024]{1,0:T(8,128)(2,1)S(1)}, u32[]{:S(2)}, u32[]{:S(2)}) collective-permute-start(f16[64,1024]{1,0:T(8,128)(2,1)S(1)} %convolution_convert_fusion), channel_id=1, source_target_pairs={{0,3},{1,2},{2,1},{3,0},{4,7},{5,6},{6,5},{7,4},{8,11},{9,10},{10,... | collective-permute-start | bytes 393224 | tf_op jit(solution)/shard_map/ppermute | solution.py:35
  29.8 7.8 %collective-permute-done.12.refs_4_ = bf16[816,128]{1,0:T(8,128)(2,1)S(1)} collective-permute-done((bf16[816,128]{1,0:T(8,128)(2,1)S(1)}, bf16[816,128]{1,0:T(8,128)(2,1)S(1)}, u32[]{:S(2)}, u32[]{:S(2)}) %collective-permute-start.12) | collective-permute-done | bytes 208928 | tf_op jit(solution)/shard_map/ppermute | solution.py:35
  37.6 2.5 %collective-permute-done.13.refs_5_ = bf16[816,128]{1,0:T(8,128)(2,1)S(1)} collective-permute-done((bf16[816,128]{1,0:T(8,128)(2,1)S(1)}, bf16[816,128]{1,0:T(8,128)(2,1)S(1)}, u32[]{:S(2)}, u32[]{:S(2)}) %collective-permute-start.13) | collective-permute-done | bytes 208928 | tf_op jit(solution)/shard_map/ppermute | solution.py:35
  40.2 0.5 collective-permute-start.2
  40.7 0.2 fusion.9
  40.9 0.1 pad_maximum_fusion
  41.0 2.2 %shard_map.116 = bf16[8,4,1024]{2,1,0:T(4,128)(2,1)} custom-call(s32[1]{0:T(128)} %bitcast.me_ref, bf16[816,128]{1,0:T(8,128)(2,1)S(1)} %get-tuple-element.18.refs_0_, bf16[816,128]{1,0:T(8,128)(2,1)S(1)} %collective-permute-done.9.refs_1_, bf16[816,128]{1,0:T(8,128)(2,1)S(1)} %collective-permute-done.10.refs_2_, ...), custom_call_target="tpu_custom_call" | custom-call | tf_op jit(solution)/shard_map/pallas_call | solution.py:378
  43.2 3.4 %all-to-all-start.1 = ((bf16[8,4,1024]{2,1,0:T(4,128)(2,1)}), bf16[8,4,1024]{2,1,0:T(4,128)(2,1)S(1)}, u32[]{:S(2)}, u32[]{:S(2)}) async-start(bf16[8,4,1024]{2,1,0:T(4,128)(2,1)} %shard_map.116), calls=%async_computation.1 | async-start | bytes 131072 | tf_op jit(solution)/shard_map/all_to_all | solution.py:385
  46.6 0.7 %collective-permute-done.2 = f16[64,1024]{1,0:T(8,128)(2,1)S(1)} collective-permute-done((f16[64,1024]{1,0:T(8,128)(2,1)S(1)}, f16[64,1024]{1,0:T(8,128)(2,1)S(1)}, u32[]{:S(2)}, u32[]{:S(2)}) %collective-permute-start.2) | collective-permute-done | bytes 131104 | tf_op jit(solution)/shard_map/ppermute | solution.py:35
  47.3 4.8 %shard_map.115 = f32[8,1,512]{2,1,0:T(1,128)} custom-call(s32[1]{0:T(128)} %bitcast.me_ref, f32[64,1024]{1,0:T(8,128)S(1)} %convert_add_fusion.projected_ref, f32[64,128]{1,0:T(8,128)S(1)} %get-tuple-element.31.cos_ref, f32[64,128]{1,0:T(8,128)S(1)} %get-tuple-element.32.sin_ref, bf16[816,128]{1,0:T(8,128)(2,1)S(1)} %get-tuple-element.18.refs_0_, ...), custom_call_target="tpu_custom_call" | custom-call | tf_op jit(solution)/shard_map/pallas_call | solution.py:393
  52.1 3.4 %all-to-all-start = ((f32[8,1,512]{2,1,0:T(1,128)}), f32[8,1,512]{2,1,0:T(1,128)S(1)}, u32[]{:S(2)}, u32[]{:S(2)}) async-start(f32[8,1,512]{2,1,0:T(1,128)} %shard_map.115), calls=%async_computation | async-start | bytes 32768 | tf_op jit(solution)/shard_map/all_to_all | solution.py:406
  55.5 4.8 %all-to-all-done = f32[8,1,512]{2,1,0:T(1,128)S(1)} async-done(((f32[8,1,512]{2,1,0:T(1,128)}), f32[8,1,512]{2,1,0:T(1,128)S(1)}, u32[]{:S(2)}, u32[]{:S(2)}) %all-to-all-start) | async-done | bytes 16416 | tf_op jit(solution)/shard_map/all_to_all | solution.py:406
  60.3 0.6 copy.12
  60.9 0.6 %copy.15 = bf16[1,4,1,8192]{3,1,2,0:T(4,128)(2,1)} copy(bf16[1,4,1,8192]{3,1,2,0:T(4,128)(2,1)S(1)} %bitcast.25) | data formatting | bytes 131072
  (21 shorter events, 0.2 us)
Async XLA Ops:
  0.6 12.3 %copy-start = (bf16[2048,1024]{1,0:T(8,128)(2,1)S(1)}, bf16[2048,1024]{1,0:T(8,128)(2,1)}, u32[]{:S(2)}) copy-start(bf16[2048,1024]{1,0:T(8,128)(2,1)} %param.11) | copy-start | bytes 12582916
  1.9 11.9 %collective-permute-start.6 = (bf16[32,2048]{1,0:T(8,128)(2,1)S(1)}, bf16[32,2048]{1,0:T(8,128)(2,1)S(1)}, u32[]{:S(2)}, u32[]{:S(2)}) collective-permute-start(bf16[32,2048]{1,0:T(8,128)(2,1)S(1)} %get-tuple-element.17), channel_id=1, source_target_pairs={{0,3},{1,2},{2,1},{3,0},{4,7},{5,6},{6,5},{7,4},{8,11},{9,10},{10,... | collective-permute-start | bytes 393224 | tf_op jit(solution)/shard_map/ppermute | solution.py:35
  7.0 11.1 %collective-permute-start.3 = (bf16[32,2048]{1,0:T(8,128)(2,1)S(1)}, bf16[32,2048]{1,0:T(8,128)(2,1)S(1)}, u32[]{:S(2)}, u32[]{:S(2)}) collective-permute-start(bf16[32,2048]{1,0:T(8,128)(2,1)S(1)} %get-tuple-element.16), channel_id=1, source_target_pairs={{0,2},{1,3},{2,0},{3,1},{4,6},{5,7},{6,4},{7,5},{8,10},{9,11},{10,... | collective-permute-start | bytes 393224 | tf_op jit(solution)/shard_map/ppermute | solution.py:35
  7.0 13.6 %collective-permute-start = (bf16[32,2048]{1,0:T(8,128)(2,1)S(1)}, bf16[32,2048]{1,0:T(8,128)(2,1)S(1)}, u32[]{:S(2)}, u32[]{:S(2)}) collective-permute-start(bf16[32,2048]{1,0:T(8,128)(2,1)S(1)} %get-tuple-element.15), channel_id=1, source_target_pairs={{0,1},{1,0},{2,3},{3,2},{4,5},{5,4},{6,7},{7,6},{8,9},{9,8},{10,11... | collective-permute-start | bytes 393224 | tf_op jit(solution)/shard_map/ppermute | solution.py:35
  11.1 13.5 %collective-permute-start.9 = (bf16[816,128]{1,0:T(8,128)(2,1)S(1)}, bf16[816,128]{1,0:T(8,128)(2,1)S(1)}, u32[]{:S(2)}, u32[]{:S(2)}) collective-permute-start(bf16[816,128]{1,0:T(8,128)(2,1)S(1)} %get-tuple-element.19), channel_id=1, source_target_pairs={{0,4},{4,0},{8,12},{12,8},{16,20},{20,16},{24,28},{28,24},{1,5},{5... | collective-permute-start | bytes 626696 | tf_op jit(solution)/shard_map/ppermute | solution.py:35
  11.2 15.0 %collective-permute-start.10 = (bf16[816,128]{1,0:T(8,128)(2,1)S(1)}, bf16[816,128]{1,0:T(8,128)(2,1)S(1)}, u32[]{:S(2)}, u32[]{:S(2)}) collective-permute-start(bf16[816,128]{1,0:T(8,128)(2,1)S(1)} %get-tuple-element.20), channel_id=1, source_target_pairs={{0,8},{4,12},{8,0},{12,4},{16,24},{20,28},{24,16},{28,20},{1,9},{5... | collective-permute-start | bytes 626696 | tf_op jit(solution)/shard_map/ppermute | solution.py:35
  13.8 4.6 %collective-permute-start.7 = (bf16[32,2048]{1,0:T(8,128)(2,1)S(1)}, bf16[32,2048]{1,0:T(8,128)(2,1)S(1)}, u32[]{:S(2)}, u32[]{:S(2)}) collective-permute-start(bf16[32,2048]{1,0:T(8,128)(2,1)S(1)} %collective-permute-done.6), channel_id=1, source_target_pairs={{0,4},{4,0},{8,12},{12,8},{16,20},{20,16},{24,28},{28,24},{1,5},{5... | collective-permute-start | bytes 393224 | tf_op jit(solution)/shard_map/ppermute | solution.py:35
  18.1 9.2 %collective-permute-start.11 = (bf16[816,128]{1,0:T(8,128)(2,1)S(1)}, bf16[816,128]{1,0:T(8,128)(2,1)S(1)}, u32[]{:S(2)}, u32[]{:S(2)}) collective-permute-start(bf16[816,128]{1,0:T(8,128)(2,1)S(1)} %get-tuple-element.21), channel_id=1, source_target_pairs={{0,12},{4,8},{8,4},{12,0},{16,28},{20,24},{24,20},{28,16},{1,13},{... | collective-permute-start | bytes 626696 | tf_op jit(solution)/shard_map/ppermute | solution.py:35
  18.4 3.8 %collective-permute-start.4 = (bf16[32,2048]{1,0:T(8,128)(2,1)S(1)}, bf16[32,2048]{1,0:T(8,128)(2,1)S(1)}, u32[]{:S(2)}, u32[]{:S(2)}) collective-permute-start(bf16[32,2048]{1,0:T(8,128)(2,1)S(1)} %collective-permute-done.3), channel_id=1, source_target_pairs={{0,4},{4,0},{8,12},{12,8},{16,20},{20,16},{24,28},{28,24},{1,5},{5... | collective-permute-start | bytes 393224 | tf_op jit(solution)/shard_map/ppermute | solution.py:35
  20.6 17.1 %collective-permute-start.12 = (bf16[816,128]{1,0:T(8,128)(2,1)S(1)}, bf16[816,128]{1,0:T(8,128)(2,1)S(1)}, u32[]{:S(2)}, u32[]{:S(2)}) collective-permute-start(bf16[816,128]{1,0:T(8,128)(2,1)S(1)} %get-tuple-element.22), channel_id=1, source_target_pairs={{0,16},{4,20},{8,24},{12,28},{16,0},{20,4},{24,8},{28,12},{1,17},{... | collective-permute-start | bytes 626696 | tf_op jit(solution)/shard_map/ppermute | solution.py:35
  22.2 1.3 %collective-permute-start.1 = (bf16[32,2048]{1,0:T(8,128)(2,1)S(1)}, bf16[32,2048]{1,0:T(8,128)(2,1)S(1)}, u32[]{:S(2)}, u32[]{:S(2)}) collective-permute-start(bf16[32,2048]{1,0:T(8,128)(2,1)S(1)} %collective-permute-done), channel_id=1, source_target_pairs={{0,4},{4,0},{8,12},{12,8},{16,20},{20,16},{24,28},{28,24},{1,5},{5... | collective-permute-start | bytes 393224 | tf_op jit(solution)/shard_map/ppermute | solution.py:35
  23.5 16.7 %collective-permute-start.13 = (bf16[816,128]{1,0:T(8,128)(2,1)S(1)}, bf16[816,128]{1,0:T(8,128)(2,1)S(1)}, u32[]{:S(2)}, u32[]{:S(2)}) collective-permute-start(bf16[816,128]{1,0:T(8,128)(2,1)S(1)} %get-tuple-element.23), channel_id=1, source_target_pairs={{0,20},{4,16},{8,28},{12,24},{16,4},{20,0},{24,12},{28,8},{1,21},{... | collective-permute-start | bytes 626696 | tf_op jit(solution)/shard_map/ppermute | solution.py:35
  24.7 16.3 %collective-permute-start.14 = (bf16[816,128]{1,0:T(8,128)(2,1)S(1)}, bf16[816,128]{1,0:T(8,128)(2,1)S(1)}, u32[]{:S(2)}, u32[]{:S(2)}) collective-permute-start(bf16[816,128]{1,0:T(8,128)(2,1)S(1)} %get-tuple-element.24), channel_id=1, source_target_pairs={{0,24},{4,28},{8,16},{12,20},{16,8},{20,12},{24,0},{28,4},{1,25},{... | collective-permute-start | bytes 626696 | tf_op jit(solution)/shard_map/ppermute | solution.py:35
  26.2 14.8 %collective-permute-start.15 = (bf16[816,128]{1,0:T(8,128)(2,1)S(1)}, bf16[816,128]{1,0:T(8,128)(2,1)S(1)}, u32[]{:S(2)}, u32[]{:S(2)}) collective-permute-start(bf16[816,128]{1,0:T(8,128)(2,1)S(1)} %get-tuple-element.25), channel_id=1, source_target_pairs={{0,28},{4,24},{8,20},{12,16},{16,12},{20,8},{24,4},{28,0},{1,29},{... | collective-permute-start | bytes 626696 | tf_op jit(solution)/shard_map/ppermute | solution.py:35
  27.3 19.2 %collective-permute-start.8 = (f16[64,1024]{1,0:T(8,128)(2,1)S(1)}, f16[64,1024]{1,0:T(8,128)(2,1)S(1)}, u32[]{:S(2)}, u32[]{:S(2)}) collective-permute-start(f16[64,1024]{1,0:T(8,128)(2,1)S(1)} %convolution_convert_fusion), channel_id=1, source_target_pairs={{0,3},{1,2},{2,1},{3,0},{4,7},{5,6},{6,5},{7,4},{8,11},{9,10},{10,... | collective-permute-start | bytes 393224 | tf_op jit(solution)/shard_map/ppermute | solution.py:35
  37.6 8.9 %collective-permute-start.5 = (f16[64,1024]{1,0:T(8,128)(2,1)S(1)}, f16[64,1024]{1,0:T(8,128)(2,1)S(1)}, u32[]{:S(2)}, u32[]{:S(2)}) collective-permute-start(f16[64,1024]{1,0:T(8,128)(2,1)S(1)} %convolution_convert_fusion.1), channel_id=1, source_target_pairs={{0,2},{1,3},{2,0},{3,1},{4,6},{5,7},{6,4},{7,5},{8,10},{9,11},{10,... | collective-permute-start | bytes 393224 | tf_op jit(solution)/shard_map/ppermute | solution.py:35
  40.2 7.1 %collective-permute-start.2 = (f16[64,1024]{1,0:T(8,128)(2,1)S(1)}, f16[64,1024]{1,0:T(8,128)(2,1)S(1)}, u32[]{:S(2)}, u32[]{:S(2)}) collective-permute-start(f16[64,1024]{1,0:T(8,128)(2,1)S(1)} %convolution_convert_fusion.2), channel_id=1, source_target_pairs={{0,1},{1,0},{2,3},{3,2},{4,5},{5,4},{6,7},{7,6},{8,9},{9,8},{10,11... | collective-permute-start | bytes 393224 | tf_op jit(solution)/shard_map/ppermute | solution.py:35
  43.2 8.9 %all-to-all-start.1 = ((bf16[8,4,1024]{2,1,0:T(4,128)(2,1)}), bf16[8,4,1024]{2,1,0:T(4,128)(2,1)S(1)}, u32[]{:S(2)}, u32[]{:S(2)}) async-start(bf16[8,4,1024]{2,1,0:T(4,128)(2,1)} %shard_map.116), calls=%async_computation.1 | async-start | bytes 131072 | tf_op jit(solution)/shard_map/all_to_all | solution.py:385
  52.1 8.2 %all-to-all-start = ((f32[8,1,512]{2,1,0:T(1,128)}), f32[8,1,512]{2,1,0:T(1,128)S(1)}, u32[]{:S(2)}, u32[]{:S(2)}) async-start(f32[8,1,512]{2,1,0:T(1,128)} %shard_map.115), calls=%async_computation | async-start | bytes 32768 | tf_op jit(solution)/shard_map/all_to_all | solution.py:406
